TPU v7x, 256 devices: a whole 4x4x8 slice. The times are simulated.
256 devices in a mesh: slab: 8 (over z), front: 32 (over y, x, core).
Axes of the slice: x: 4, y: 4, z: 8, core: 2. Of those that a mesh axis runs over, the one named last changes fastest.
Arguments:
- leaf_rhs: bfloat16 [8, 2, 512, 128, 512], P('slab', None, 'front'), may hold values from -6 to 6
- leaf_inv: bfloat16 [8, 512, 2, 128, 128], P('slab', 'front'), may hold values from -0.375 to 0.375
- leaf_off: bfloat16 [8, 512, 2, 128, 128], P('slab', 'front'), may hold values from -0.125 to 0.125
- parent: int32 [8, 512, 1], P('slab', 'front'), may hold values from 0 to 31; in each aligned block of 16 rows (0 to 15, 16 to 31, ..., all dimensions but the last counted through in order) no two rows name the same one
- ancestors: int32 [8, 512, 128], P('slab', 'front'), may hold values from 0 to 255
- root_rhs: bfloat16 [8, 2, 8192, 512], P('slab', None, 'front'), may hold values from -6 to 6
- root_inv: float32 [8, 64, 2, 128, 128], P('slab', 'front'), may hold values from -2 to 2.5
- coupling: float32 [8, 8192], P('slab', 'front'), may hold values from 0.6 to 1.3
Outputs:
- leaf_sol: bfloat16 [8, 2, 512, 128, 512], P('slab', None, 'front')
- root_sol: float32 [8, 2, 8192, 512], P('slab', None, 'front')
Inputs may be any that keep to these rules, and one draw needn't show every extreme that they name: Each front index's 16 leaf blocks of a slab name any one parent at most 1 times. `ancestors`: rows may repeat within a block.
All inputs are finite; a program needn't handle non-finite values.
Results may differ from a plain program's by a relative error of at most 0.0057.
Values may be sent and summed in bfloat16 or wider, within the bound.
A program may use at most 128 MiB of HBM per device.

v0:
```python
import jax
import jax.numpy as jnp
from jax import lax
from jax.sharding import PartitionSpec as P


def passed_along(x, axis, by):
    count = lax.axis_size(axis)
    pairs = [(i, i + by) for i in range(count) if 0 <= i + by < count]
    return lax.ppermute(x, axis, pairs)


def planes_apply(real_mat, imag_mat, real_vec, imag_vec, form):
    real = jnp.einsum(form, real_mat, real_vec, preferred_element_type=jnp.float32) - jnp.einsum(
        form, imag_mat, imag_vec, preferred_element_type=jnp.float32
    )
    imag = jnp.einsum(form, real_mat, imag_vec, preferred_element_type=jnp.float32) + jnp.einsum(
        form, imag_mat, real_vec, preferred_element_type=jnp.float32
    )
    return jnp.stack([real, imag])


def block_solve(blocks, field):
    highest = lax.Precision.HIGHEST
    shaped = field.reshape(2, blocks.shape[0], blocks.shape[2], field.shape[-1])
    real = jnp.einsum("kij,kjc->kic", blocks[:, 0], shaped[0], precision=highest) - jnp.einsum(
        "kij,kjc->kic", blocks[:, 1], shaped[1], precision=highest
    )
    imag = jnp.einsum("kij,kjc->kic", blocks[:, 0], shaped[1], precision=highest) + jnp.einsum(
        "kij,kjc->kic", blocks[:, 1], shaped[0], precision=highest
    )
    return jnp.stack([real, imag]).reshape(field.shape)


def body(leaf_rhs, leaf_inv, leaf_off, parent, ancestors, root_rhs, root_inv, coupling):
    forward_form = "lij,ljc->lic"
    back_form = "lji,ljc->lic"
    rhs = leaf_rhs[0]
    inverse = leaf_inv[0]
    offdiag = leaf_off[0]
    owners = parent[0, :, 0]
    anc_rows = ancestors[0]
    fronts = lax.axis_size("front")
    count = owners.shape[0]
    per_owner = (count + fronts - 1) // fronts
    blk = rhs.shape[2]
    width = rhs.shape[3]
    root_rows = root_rhs.shape[2]
    slot_total = fronts * per_owner
    hits = (owners[:, None] == jnp.arange(fronts, dtype=jnp.int32)[None, :]).astype(jnp.int32)
    rank = jnp.sum((jnp.cumsum(hits, axis=0) - hits) * hits, axis=1)
    slot = owners * per_owner + rank
    place_int = (slot[:, None] == jnp.arange(slot_total, dtype=jnp.int32)[None, :]).astype(
        jnp.int32
    )
    place = place_int.astype(jnp.bfloat16)
    slot_ids = jnp.sum(place_int[:, :, None] * anc_rows[:, None, :], axis=0).reshape(
        1, fronts, per_owner, blk
    )
    forward = planes_apply(inverse[:, 0], inverse[:, 1], rhs[0], rhs[1], forward_form).astype(
        jnp.bfloat16
    )
    partial_value = planes_apply(
        offdiag[:, 0], offdiag[:, 1], forward[0], forward[1], forward_form
    ).astype(jnp.bfloat16)
    placed = jnp.einsum(
        "ks,pkbc->psbc", place, partial_value, preferred_element_type=jnp.float32
    ).astype(jnp.bfloat16)
    placed = placed.reshape(2, fronts, per_owner, blk, width)
    arrived, arrived_ids = (
        lax.all_to_all(placed, "front", split_axis=1, concat_axis=1, tiled=True),
        lax.all_to_all(slot_ids, "front", split_axis=1, concat_axis=1, tiled=True),
    )
    slot_parts = arrived.reshape(2, slot_total * blk, width)
    flat_ids = arrived_ids.reshape(-1)
    row_table = (flat_ids[:, None] == jnp.arange(root_rows, dtype=jnp.int32)[None, :]).astype(
        jnp.bfloat16
    )
    summed = jnp.einsum("sr,psc->prc", row_table, slot_parts, preferred_element_type=jnp.float32)
    reduced = root_rhs[0].astype(jnp.float32) - summed
    blocks = root_inv[0]
    cpl = coupling[0]
    first = block_solve(blocks, reduced)

    def relay(step, state):
        previous = passed_along(state, "slab", 1)
        return block_solve(blocks, reduced - cpl[None, :, None] * previous)

    state = lax.fori_loop(0, lax.axis_size("slab") - 1, relay, first)
    root_half = state.astype(jnp.bfloat16)
    slot_rows = jnp.einsum(
        "sr,prc->psc", row_table, root_half, preferred_element_type=jnp.float32
    ).astype(jnp.bfloat16)
    slot_rows = slot_rows.reshape(2, fronts, per_owner, blk, width)
    returned = lax.all_to_all(slot_rows, "front", split_axis=1, concat_axis=1, tiled=True)
    picked = jnp.einsum(
        "ks,psbc->pkbc",
        place,
        returned.reshape(2, slot_total, blk, width),
        preferred_element_type=jnp.float32,
    ).astype(jnp.bfloat16)
    back = planes_apply(offdiag[:, 0], offdiag[:, 1], picked[0], picked[1], back_form).astype(
        jnp.bfloat16
    )
    solved = forward.astype(jnp.float32) - planes_apply(
        inverse[:, 0], inverse[:, 1], back[0], back[1], forward_form
    )
    return (solved.astype(jnp.bfloat16)[None], state[None])


def solution(mesh):
    in_specs = (
        P("slab", None, "front", None, None),
        P("slab", "front", None, None, None),
        P("slab", "front", None, None, None),
        P("slab", "front", None),
        P("slab", "front", None),
        P("slab", None, "front", None),
        P("slab", "front", None, None, None),
        P("slab", "front"),
    )
    out_specs = (P("slab", None, "front", None, None), P("slab", None, "front", None))
    return jax.shard_map(body, mesh=mesh, in_specs=in_specs, out_specs=out_specs, check_vma=False)
```

profile of v0, /device:TPU:129, one launch (start us, length us, event | category | flops | bytes accessed | tf_op | source)
XLA Modules:
  0.0 566.3 jit_solution(2342361114886660467)
XLA Ops:
  2.1 4.8 fusion.20
  6.9 2.7 fusion.24
  10.0 3.9 add_convert_fusion.2
  19.8 2.4 pad_maximum_fusion.1
  22.2 8.3 %copy.77 = bf16[2,16,128,512]{3,1,2,0:T(8,128)(2,1)} copy(bf16[2,16,128,512]{2,3,1,0:T(8,128)(2,1)} %pad_maximum_fusion.1) | data formatting | bytes 8388608 | tf_op jit(solution)/shard_map/stack | solution.py:20
  30.6 7.9 %convert_bitcast_fusion = bf16[2,32,1,128,512]{4,1,3,0,2:T(8,128)(2,1)} fusion(bf16[2,16,128,512]{3,1,2,0:T(8,128)(2,1)} %copy.77, s32[16]{0:T(128)S(1)} %bitcast_add_fusion), kind=kOutput, calls=%fused_computation.19 | convolution fusion | flops 138413568 | bytes 12582976 | tf_op jit(solution)/shard_map/ks,pkbc->psbc/dot_general | solution.py:66
  38.4 11.4 %copy.78 = bf16[2,32,1,128,512]{4,3,0,2,1:T(8,128)(2,1)} copy(bf16[2,32,1,128,512]{4,1,3,0,2:T(8,128)(2,1)} %convert_bitcast_fusion) | data formatting | bytes 16777216 | tf_op jit(solution)/shard_map/reshape | solution.py:69
  49.8 8.0 %all-to-all-start = ((bf16[2,32,1,128,512]{4,3,0,2,1:T(8,128)(2,1)}), bf16[2,32,1,128,512]{4,3,0,2,1:T(8,128)(2,1)}, u32[]{:S(2)}, u32[]{:S(2)}) async-start(bf16[2,32,1,128,512]{4,3,0,2,1:T(8,128)(2,1)} %copy.78), calls=%async_computation | async-start | bytes 16777216 | tf_op jit(solution)/shard_map/all_to_all | solution.py:71
  58.6 99.9 %all-to-all-done = bf16[2,32,1,128,512]{4,3,0,2,1:T(8,128)(2,1)} async-done(((bf16[2,32,1,128,512]{4,3,0,2,1:T(8,128)(2,1)}), bf16[2,32,1,128,512]{4,3,0,2,1:T(8,128)(2,1)}, u32[]{:S(2)}, u32[]{:S(2)}) %all-to-all-start) | async-done | bytes 8388640 | tf_op jit(solution)/shard_map/all_to_all | solution.py:71
  158.4 9.2 %all-to-all-start.1 = ((s32[1,32,1,128]{3,2,0,1:T(1,128)}), s32[1,32,1,128]{3,2,0,1:T(1,128)S(1)}, u32[]{:S(2)}, u32[]{:S(2)}) async-start(s32[1,32,1,128]{3,2,0,1:T(1,128)} %bitcast.32), calls=%async_computation.1 | async-start | bytes 32768 | tf_op jit(solution)/shard_map/all_to_all | solution.py:72
  167.7 7.6 %copy.79 = bf16[2,32,1,128,512]{4,3,1,0,2:T(8,128)(2,1)} copy(bf16[2,32,1,128,512]{4,3,0,2,1:T(8,128)(2,1)} %all-to-all-done) | data formatting | bytes 16777216 | tf_op jit(solution)/shard_map/all_to_all | solution.py:71
  175.3 6.7 %fusion.37 = f32[2,256,512]{2,1,0:T(8,128)S(1)} fusion(bf16[2,4096,512]{2,1,0:T(8,128)(2,1)} %bitcast.229, s32[4096]{0:T(1024)S(1)} %bitcast.237, bf16[1,2,256,512]{3,2,1,0:T(8,128)(2,1)} %param.15), kind=kOutput, calls=%fused_computation.51 | convolution fusion | flops 2149056512 | bytes 9977856 | tf_op jit(solution)/shard_map/sr,psc->prc/dot_general | solution.py:79
  185.6 212.0 %while.10 = (s32[]{:T(128)}, f32[2,256,512]{2,1,0:T(8,128)}, f32[1,256]{1,0:T(1,128)S(1)}, f32[2,256,512]{2,1,0:T(8,128)S(1)}, f32[2,2,128,128]{3,2,0,1:T(8,128)S(1)}, /*index=5*/s32[]{:T(128)}) while((s32[]{:T(128)}, f32[2,256,512]{2,1,0:T(8,128)}, f32[1,256]{1,0:T(1,128)S(1)}, f32[2,256,512]{2,1,0:T(8,128)S(1)}, ...), condition=%wide.region_4.5_spmd, body=%wide.region_3.4_spmd.sunk | while | flops 806354944 | bytes 17302636 | solution.py:89
  185.6 2.6 collective-permute-start
  188.2 25.3 %collective-permute-done = f32[2,256,512]{2,1,0:T(8,128)} collective-permute-done((f32[2,256,512]{2,1,0:T(8,128)}, f32[2,256,512]{2,1,0:T(8,128)}, u32[]{:S(2)}, u32[]{:S(2)}) %collective-permute-start) | collective-permute-done | bytes 1048608 | tf_op jit(solution)/shard_map/while/body/eval_jaxpr/ppermute | solution.py:10
  218.4 1.9 collective-permute-start
  220.4 25.1 %collective-permute-done = f32[2,256,512]{2,1,0:T(8,128)} collective-permute-done((f32[2,256,512]{2,1,0:T(8,128)}, f32[2,256,512]{2,1,0:T(8,128)}, u32[]{:S(2)}, u32[]{:S(2)}) %collective-permute-start) | collective-permute-done | bytes 1048608 | tf_op jit(solution)/shard_map/while/body/eval_jaxpr/ppermute | solution.py:10
  252.4 24.3 %collective-permute-done = f32[2,256,512]{2,1,0:T(8,128)} collective-permute-done((f32[2,256,512]{2,1,0:T(8,128)}, f32[2,256,512]{2,1,0:T(8,128)}, u32[]{:S(2)}, u32[]{:S(2)}) %collective-permute-start) | collective-permute-done | bytes 1048608 | tf_op jit(solution)/shard_map/while/body/eval_jaxpr/ppermute | solution.py:10
  283.5 23.4 %collective-permute-done = f32[2,256,512]{2,1,0:T(8,128)} collective-permute-done((f32[2,256,512]{2,1,0:T(8,128)}, f32[2,256,512]{2,1,0:T(8,128)}, u32[]{:S(2)}, u32[]{:S(2)}) %collective-permute-start) | collective-permute-done | bytes 1048608 | tf_op jit(solution)/shard_map/while/body/eval_jaxpr/ppermute | solution.py:10
  313.8 22.6 %collective-permute-done = f32[2,256,512]{2,1,0:T(8,128)} collective-permute-done((f32[2,256,512]{2,1,0:T(8,128)}, f32[2,256,512]{2,1,0:T(8,128)}, u32[]{:S(2)}, u32[]{:S(2)}) %collective-permute-start) | collective-permute-done | bytes 1048608 | tf_op jit(solution)/shard_map/while/body/eval_jaxpr/ppermute | solution.py:10
  343.2 21.7 %collective-permute-done = f32[2,256,512]{2,1,0:T(8,128)} collective-permute-done((f32[2,256,512]{2,1,0:T(8,128)}, f32[2,256,512]{2,1,0:T(8,128)}, u32[]{:S(2)}, u32[]{:S(2)}) %collective-permute-start) | collective-permute-done | bytes 1048608 | tf_op jit(solution)/shard_map/while/body/eval_jaxpr/ppermute | solution.py:10
  371.8 20.8 %collective-permute-done = f32[2,256,512]{2,1,0:T(8,128)} collective-permute-done((f32[2,256,512]{2,1,0:T(8,128)}, f32[2,256,512]{2,1,0:T(8,128)}, u32[]{:S(2)}, u32[]{:S(2)}) %collective-permute-start) | collective-permute-done | bytes 1048608 | tf_op jit(solution)/shard_map/while/body/eval_jaxpr/ppermute | solution.py:10
  397.6 6.7 %convolution_convert_fusion = bf16[2,512,4096]{2,1,0:T(8,128)(2,1)} fusion(s32[4096]{0:T(1024)S(1)} %bitcast.238, f32[2,256,512]{2,1,0:T(8,128)} %get-tuple-element.29), kind=kOutput, calls=%fused_computation.20 | convolution fusion | flops 2152988672 | bytes 9453568 | tf_op jit(solution)/shard_map/sr,prc->psc/dot_general | solution.py:91
  404.3 9.4 %copy.106 = bf16[128,8,32,128]{3,2,1,0:T(8,128)(2,1)} copy(bf16[128,8,32,128]{3,1,2,0:T(8,128)(2,1)} %bitcast.209) | data formatting | bytes 16777216
  413.7 14.0 %copy.84 = bf16[2,32,1,128,512]{4,3,0,2,1:T(8,128)(2,1)} copy(bf16[2,32,1,128,512]{3,1,4,0,2:T(8,128)(2,1)} %bitcast.210) | data formatting | bytes 16777216 | tf_op jit(solution)/shard_map/reshape | solution.py:94
  427.7 108.1 %all_to_all.15 = bf16[2,32,1,128,512]{4,3,0,2,1:T(8,128)(2,1)S(1)} all-to-all(bf16[2,32,1,128,512]{4,3,0,2,1:T(8,128)(2,1)} %copy.84), channel_id=1, replica_groups=mesh['slab'=8,'front'=32] {'front'}, dimensions={1} | all-to-all | bytes 16777216 | tf_op jit(solution)/shard_map/all_to_all | solution.py:95
  535.8 5.9 %convert_bitcast_fusion.1 = bf16[2,16,128,512]{3,1,2,0:T(8,128)(2,1)S(1)} fusion(bf16[2,32,1,128,512]{4,3,0,2,1:T(8,128)(2,1)S(1)} %all_to_all.15, s32[16]{0:T(128)S(1)} %bitcast_add_fusion), kind=kOutput, calls=%fused_computation.26 | convolution fusion | flops 136316416 | bytes 12582976 | tf_op jit(solution)/shard_map/ks,psbc->pkbc/dot_general | solution.py:96
  541.7 2.5 slice_bitcast_fusion.1
  544.2 4.7 copy.86
  548.8 4.5 copy.87
  553.3 2.4 fusion.43
  563.1 3.0 fusion.10
  (114 shorter events, 63.3 us)
Async XLA Ops:
  0.6 6.3 %copy-start.8 = (bf16[1,2,16,128,512]{4,3,2,1,0:T(8,128)(2,1)S(1)}, bf16[1,2,16,128,512]{4,3,2,1,0:T(8,128)(2,1)}, u32[]{:S(2)}) copy-start(bf16[1,2,16,128,512]{4,3,2,1,0:T(8,128)(2,1)} %param.10) | copy-start | bytes 12582916
  2.1 11.8 %copy-start.4 = (bf16[1,16,2,128,128]{4,3,1,2,0:T(8,128)(2,1)}, bf16[1,16,2,128,128]{4,3,1,2,0:T(8,128)(2,1)S(1)}, u32[]{:S(2)}) copy-start(bf16[1,16,2,128,128]{4,3,1,2,0:T(8,128)(2,1)S(1)} %copy.117) | copy-start | bytes 3145732
  6.9 2.7 copy-start.15
  6.9 3.0 copy-start.11
  10.0 8.9 %copy-start.2 = (bf16[1,16,2,128,128]{4,3,1,2,0:T(8,128)(2,1)}, bf16[1,16,2,128,128]{4,3,1,2,0:T(8,128)(2,1)S(1)}, u32[]{:S(2)}) copy-start(bf16[1,16,2,128,128]{4,3,1,2,0:T(8,128)(2,1)S(1)} %copy.116) | copy-start | bytes 3145732
  10.0 4.4 copy-start.9
  10.0 5.7 copy-start.10
  16.4 1.6 copy-start
  49.8 8.0 %copy-start.14 = (s32[1,16,128]{2,1,0:T(8,128)S(1)}, s32[1,16,128]{2,1,0:T(8,128)}, u32[]{:S(2)}) copy-start(s32[1,16,128]{2,1,0:T(8,128)} %param.14) | copy-start | bytes 24580
  49.8 117.9 %copy-start.12 = (f32[1,2,2,128,128]{4,3,2,1,0:T(8,128)S(1)}, f32[1,2,2,128,128]{4,3,2,1,0:T(8,128)}, u32[]{:S(2)}) copy-start(f32[1,2,2,128,128]{4,3,2,1,0:T(8,128)} %param.16) | copy-start | bytes 786436
  49.8 108.7 %all-to-all-start = ((bf16[2,32,1,128,512]{4,3,0,2,1:T(8,128)(2,1)}), bf16[2,32,1,128,512]{4,3,0,2,1:T(8,128)(2,1)}, u32[]{:S(2)}, u32[]{:S(2)}) async-start(bf16[2,32,1,128,512]{4,3,0,2,1:T(8,128)(2,1)} %copy.78), calls=%async_computation | async-start | bytes 16777216 | tf_op jit(solution)/shard_map/all_to_all | solution.py:71
  158.4 16.9 %all-to-all-start.1 = ((s32[1,32,1,128]{3,2,0,1:T(1,128)}), s32[1,32,1,128]{3,2,0,1:T(1,128)S(1)}, u32[]{:S(2)}, u32[]{:S(2)}) async-start(s32[1,32,1,128]{3,2,0,1:T(1,128)} %bitcast.32), calls=%async_computation.1 | async-start | bytes 32768 | tf_op jit(solution)/shard_map/all_to_all | solution.py:72
  182.1 3.5 copy-start.13
  185.6 27.9 %collective-permute-start = (f32[2,256,512]{2,1,0:T(8,128)}, f32[2,256,512]{2,1,0:T(8,128)}, u32[]{:S(2)}, u32[]{:S(2)}) collective-permute-start(f32[2,256,512]{2,1,0:T(8,128)} %get-tuple-element.88), channel_id=1, source_target_pairs={{0,32},{32,64},{64,96},{96,128},{128,160},{160,192},{192,224},{1,3... | collective-permute-start | bytes 3145736 | tf_op jit(solution)/shard_map/while/body/eval_jaxpr/ppermute | solution.py:10
  218.4 27.0 %collective-permute-start = (f32[2,256,512]{2,1,0:T(8,128)}, f32[2,256,512]{2,1,0:T(8,128)}, u32[]{:S(2)}, u32[]{:S(2)}) collective-permute-start(f32[2,256,512]{2,1,0:T(8,128)} %get-tuple-element.88), channel_id=1, source_target_pairs={{0,32},{32,64},{64,96},{96,128},{128,160},{160,192},{192,224},{1,3... | collective-permute-start | bytes 3145736 | tf_op jit(solution)/shard_map/while/body/eval_jaxpr/ppermute | solution.py:10
  250.4 26.2 %collective-permute-start = (f32[2,256,512]{2,1,0:T(8,128)}, f32[2,256,512]{2,1,0:T(8,128)}, u32[]{:S(2)}, u32[]{:S(2)}) collective-permute-start(f32[2,256,512]{2,1,0:T(8,128)} %get-tuple-element.88), channel_id=1, source_target_pairs={{0,32},{32,64},{64,96},{96,128},{128,160},{160,192},{192,224},{1,3... | collective-permute-start | bytes 3145736 | tf_op jit(solution)/shard_map/while/body/eval_jaxpr/ppermute | solution.py:10
  281.6 25.3 %collective-permute-start = (f32[2,256,512]{2,1,0:T(8,128)}, f32[2,256,512]{2,1,0:T(8,128)}, u32[]{:S(2)}, u32[]{:S(2)}) collective-permute-start(f32[2,256,512]{2,1,0:T(8,128)} %get-tuple-element.88), channel_id=1, source_target_pairs={{0,32},{32,64},{64,96},{96,128},{128,160},{160,192},{192,224},{1,3... | collective-permute-start | bytes 3145736 | tf_op jit(solution)/shard_map/while/body/eval_jaxpr/ppermute | solution.py:10
  311.9 24.5 %collective-permute-start = (f32[2,256,512]{2,1,0:T(8,128)}, f32[2,256,512]{2,1,0:T(8,128)}, u32[]{:S(2)}, u32[]{:S(2)}) collective-permute-start(f32[2,256,512]{2,1,0:T(8,128)} %get-tuple-element.88), channel_id=1, source_target_pairs={{0,32},{32,64},{64,96},{96,128},{128,160},{160,192},{192,224},{1,3... | collective-permute-start | bytes 3145736 | tf_op jit(solution)/shard_map/while/body/eval_jaxpr/ppermute | solution.py:10
  341.3 23.6 %collective-permute-start = (f32[2,256,512]{2,1,0:T(8,128)}, f32[2,256,512]{2,1,0:T(8,128)}, u32[]{:S(2)}, u32[]{:S(2)}) collective-permute-start(f32[2,256,512]{2,1,0:T(8,128)} %get-tuple-element.88), channel_id=1, source_target_pairs={{0,32},{32,64},{64,96},{96,128},{128,160},{160,192},{192,224},{1,3... | collective-permute-start | bytes 3145736 | tf_op jit(solution)/shard_map/while/body/eval_jaxpr/ppermute | solution.py:10
  369.9 22.8 %collective-permute-start = (f32[2,256,512]{2,1,0:T(8,128)}, f32[2,256,512]{2,1,0:T(8,128)}, u32[]{:S(2)}, u32[]{:S(2)}) collective-permute-start(f32[2,256,512]{2,1,0:T(8,128)} %get-tuple-element.88), channel_id=1, source_target_pairs={{0,32},{32,64},{64,96},{96,128},{128,160},{160,192},{192,224},{1,3... | collective-permute-start | bytes 3145736 | tf_op jit(solution)/shard_map/while/body/eval_jaxpr/ppermute | solution.py:10
  544.2 9.2 %copy-start.3 = (bf16[1,16,2,128,128]{4,3,1,2,0:T(8,128)(2,1)S(1)}, bf16[1,16,2,128,128]{4,3,1,2,0:T(8,128)(2,1)}, u32[]{:S(2)}) copy-start(bf16[1,16,2,128,128]{4,3,1,2,0:T(8,128)(2,1)} %copy-done.2) | copy-start | bytes 3145732
  553.3 2.4 copy-start.7
  556.5 1.6 copy-start.6
  558.1 1.2 copy-start.5
  561.5 1.6 copy-start.1
where the time goes:
time: 573 us; the launch traced here: 566 us
  waiting for transfers between devices  263 us (46%)
  blocking collectives  108 us (19%)
  matrix products  69.3 us (12%)
  local copies, waits for them, and re-layouts  68.5 us (12%)
  starting transfers between devices  31.3 us (5%)
  other arithmetic  24.5 us (4%)
    ppermute x7, waiting for transfers between devices, passed_along(): return lax.ppermute(x, axis, pairs)  163 us
    all_to_all x1, blocking collectives, body(): lax.all_to_all(slot_rows, 'front', split_axis=1, concat_axis=1, tiled=True)  108 us
    all_to_all x1, waiting for transfers between devices, body(): lax.all_to_all(placed, 'front', split_axis=1, concat_axis=1, tiled=True)  99.9 us
    unnamed x36, local copies, waits for them, and re-layouts  15 us
    ppermute x7, starting transfers between devices, passed_along(): return lax.ppermute(x, axis, pairs)  14.1 us
    reshape x1, local copies, waits for them, and re-layouts, body(): slot_rows = slot_rows.reshape(2, fronts, per_owner, blk, width)  14 us
  transfers between devices with their start and end apart: 9, of which 8 were waited for; matrix products, arithmetic and copies ran while one was open for 1% of the time, Pallas kernels for 0%

commit v1 on v0

v1 whole, which is shorter than its diff:
```python
import jax
import jax.numpy as jnp
from jax import lax
from jax.experimental import pallas as pl
from jax.experimental.pallas import tpu as pltpu
from jax.sharding import PartitionSpec as P

BF = jnp.bfloat16
F32 = jnp.float32
B = 128
C = 128
LEAF = 16
RING = 4
SLOTS = RING * RING
MESSAGES = 52
LAG_NUM, LAG_DEN = 3, 8
STEPS_AFTER = 10


def dot(a, b):
    return jnp.dot(a, b, preferred_element_type=F32)


def widened(real, imag):
    top = jnp.concatenate([real, -imag], axis=1)
    low = jnp.concatenate([imag, real], axis=1)
    return jnp.concatenate([top, low], axis=0)


def kernel(
    slot_leaf, leaf_slot, rhs, inv, off, ids, root_rhs, root_inv, cpl,
    sol_out, root_out,
    X, PART, SND, RCV, IDR, T, TT, OFFT, E, A1, F1, R1, A2, F2, RR, AH, AL, Z, Y, G, RCB, STAGE,
    ssem, rsem, idsem, insem, rrsem, outsem, rootsem,
):
    slabs = lax.axis_size("slab")
    chunks = X.shape[0]
    slab = lax.axis_index("slab")
    front = lax.axis_index("front")
    core = front % 2
    chip = front // 2
    cx = chip % RING
    cy = chip // RING

    def at(x, y, c):
        return (slab, (y * RING + x) * 2 + c)

    partner = at(cx, cy, 1 - core)
    x_next = at((cx + 1) % RING, cy, core)
    x_prev = at((cx + RING - 1) % RING, cy, core)
    y_next = at(cx, (cy + 1) % RING, core)
    y_prev = at(cx, (cy + RING - 1) % RING, core)
    z_next = ((slab + 1) % slabs, front)
    z_prev = ((slab + slabs - 1) % slabs, front)
    ways = ((x_next, x_prev), (y_next, y_prev))

    barrier = pltpu.get_barrier_semaphore()
    for device in (partner, x_next, x_prev, y_next, y_prev, z_next, z_prev):
        pl.semaphore_signal(barrier, inc=1, device_id=device, device_id_type=pl.DeviceIdType.MESH)

    def cols(k):
        return pl.ds(pl.multiple_of(k * C, C), C)

    def rhs_in(k):
        return pltpu.make_async_copy(rhs.at[0, :, :, :, cols(k)], X.at[k], insem.at[k])

    def root_rhs_in(k):
        return pltpu.make_async_copy(root_rhs.at[0, :, :, cols(k)], RR.at[k], rrsem.at[k])

    def sol_back(k):
        return pltpu.make_async_copy(X.at[k], sol_out.at[0, :, :, :, cols(k)], outsem.at[k])

    def root_back(k):
        return pltpu.make_async_copy(Y.at[k], root_out.at[0, :, :, cols(k)], rootsem.at[k])

    for k in range(chunks):
        rhs_in(k).start()
        root_rhs_in(k).start()

    def send(src, dst, k, m, device):
        return pltpu.make_async_remote_copy(
            src_ref=src, dst_ref=dst, send_sem=ssem.at[k, m], recv_sem=rsem.at[k, m],
            device_id=device, device_id_type=pl.DeviceIdType.MESH,
        )

    def ids_copy():
        return pltpu.make_async_remote_copy(
            src_ref=ids.at[1], dst_ref=IDR, send_sem=idsem.at[0], recv_sem=idsem.at[1],
            device_id=partner, device_id_type=pl.DeviceIdType.MESH,
        )

    def part_copy(k):
        return send(SND.at[k], RCV.at[k], k, 0, partner)

    def rs_copy(k, p, phase, m):
        nxt, prv = ways[p if phase == 0 else 1 - p]
        if phase == 0:
            src, mid, fin = E, A1, F1
        else:
            src, mid, fin = R1, A2, F2
        s, d, device = (
            (src.at[k, p, 2, 0], mid.at[k, p, 0], nxt),
            (src.at[k, p, 1, 1], fin.at[k, p, 0, 1], nxt),
            (src.at[k, p, 1, 0], fin.at[k, p, 0, 0], nxt),
            (src.at[k, p, 2, 1], mid.at[k, p, 1], prv),
            (src.at[k, p, 3, 0], fin.at[k, p, 1, 0], prv),
            (src.at[k, p, 3, 1], fin.at[k, p, 1, 1], prv),
        )[m]
        return send(s, d, k, 1 + phase * 12 + p * 6 + m, device)

    def sweep_copy(k, b):
        return send(G.at[k, :, 0, b, 0], Z.at[k, b], k, 25 + b, z_next)

    def ag_copy(k, p, phase, m):
        nxt, prv = ways[1 - p if phase == 0 else p]
        if phase == 0:
            def g(r, h):
                return G.at[k, p, 0, h, r]
        else:
            def g(r, h):
                return G.at[k, p, r, h]
        s, d, device = (
            (g(0, 0), g(3, 0), nxt),
            (g(0, 1), g(3, 1), nxt),
            (g(3, 0), g(2, 0), nxt),
            (g(0, 1), g(1, 1), prv),
            (g(0, 0), g(1, 0), prv),
            (g(1, 1), g(2, 1), prv),
        )[m]
        return send(s, d, k, 27 + phase * 12 + p * 6 + m, device)

    def pick_copy(k):
        return send(SND.at[k], RCB.at[k], k, 51, partner)

    @pl.when(slab == 0)
    def _():
        Z[...] = jnp.zeros_like(Z)

    pl.semaphore_wait(barrier, 7)
    ids_copy().start()

    for b in range(2):
        full = widened(root_inv[0, b, 0], root_inv[0, b, 1])
        high = full.astype(BF)
        AH[b] = high
        AL[b] = (full - high.astype(F32)).astype(BF)

    def fwd(k):
        rhs_in(k).wait()
        par = k % 2

        def leaf(l, carry):
            v = jnp.concatenate([X[k, 0, l], X[k, 1, l]], axis=0)
            f = dot(widened(inv[0, l, 0], inv[0, l, 1]), v).astype(BF)
            X[k, 0, l] = f[:B]
            X[k, 1, l] = f[B:]
            w = dot(widened(off[0, l, 0], off[0, l, 1]), f).astype(BF)
            PART[par, l, 0] = w[:B]
            PART[par, l, 1] = w[B:]
            return carry

        lax.fori_loop(0, LEAF, leaf, 0, unroll=2)

        def put(q, carry):
            SND[k, q] = PART[par, slot_leaf[SLOTS + q]]
            return carry

        lax.fori_loop(0, SLOTS, put, 0, unroll=2)
        part_copy(k).start()

    def setup_tables():
        ids_copy().wait_recv()

        def table(q, carry):
            both = jnp.concatenate([ids[0, pl.ds(q, 1), :], IDR[pl.ds(q, 1), :]], axis=1)
            rows = lax.broadcasted_iota(jnp.int32, (2 * B, 2 * B), 0)
            T[q] = jnp.where(rows == jnp.broadcast_to(both, (2 * B, 2 * B)), 1.0, 0.0).astype(BF)
            return carry

        lax.fori_loop(0, SLOTS, table, 0)

    def setup_transposed():
        def table(q, carry):
            TT[q] = T[q].astype(F32).T.astype(BF)
            OFFT[q] = widened(off[0, q, 0].astype(F32).T, off[0, q, 1].astype(F32).T).astype(BF)
            return carry

        lax.fori_loop(0, SLOTS, table, 0)

    def expand(k):
        part_copy(k).wait_recv()
        par = k % 2

        def slot(q, carry):
            rx, ry = q // RING, q % RING
            leaf = slot_leaf[q]
            v = jnp.concatenate(
                [
                    jnp.concatenate([PART[par, leaf, 0], PART[par, leaf, 1]], axis=1),
                    jnp.concatenate([RCV[k, q, 0], RCV[k, q, 1]], axis=1),
                ],
                axis=0,
            )
            e = dot(T[q], v).astype(BF)
            E[k, 0, rx, 0, ry] = e[:B, :C]
            E[k, 0, rx, 1, ry] = e[B:, :C]
            E[k, 1, ry, 0, rx] = e[:B, C:]
            E[k, 1, ry, 1, rx] = e[B:, C:]
            return carry

        lax.fori_loop(0, SLOTS, slot, 0, unroll=2)
        for m in (0, 3, 1, 4):
            for p in range(2):
                rs_copy(k, p, 0, m).start()

    def rs_relay_first(k):
        for m, r, h, d in ((0, 1, 0, 0), (3, 3, 1, 1)):
            for p in range(2):
                rs_copy(k, p, 0, m).wait_recv()
                for i in range(RING):
                    E[k, p, r, h, i] = (
                        E[k, p, r, h, i].astype(F32) + A1[k, p, d, i].astype(F32)
                    ).astype(BF)
                rs_copy(k, p, 0, 2 if d == 0 else 5).start()

    def rs_turn(k):
        for p in range(2):
            for m in (1, 4, 2, 5):
                rs_copy(k, p, 0, m).wait_recv()
            for r in (2, 1, 3, 0):
                for h in range(2):
                    R1[k, p, r, h] = (
                        E[k, p, 0, h, r].astype(F32)
                        + F1[k, p, 0, h, r].astype(F32)
                        + F1[k, p, 1, h, r].astype(F32)
                    ).astype(BF)
            for m in (0, 3, 1, 4):
                rs_copy(k, p, 1, m).start()

    def rs_relay_second(k):
        for m, r, h, d in ((0, 1, 0, 0), (3, 3, 1, 1)):
            for p in range(2):
                rs_copy(k, p, 1, m).wait_recv()
                R1[k, p, r, h] = (
                    R1[k, p, r, h].astype(F32) + A2[k, p, d].astype(F32)
                ).astype(BF)
                rs_copy(k, p, 1, 2 if d == 0 else 5).start()

    def sweep(k):
        root_rhs_in(k).wait()
        for p in range(2):
            for m in (1, 4, 2, 5):
                rs_copy(k, p, 1, m).wait_recv()
        for b in range(2):
            right = []
            for p in range(2):
                total = (
                    R1[k, p, 0, b].astype(F32)
                    + F2[k, p, 0, b].astype(F32)
                    + F2[k, p, 1, b].astype(F32)
                )
                right.append(RR[k, p, pl.ds(b * B, B), :].astype(F32) - total)

            @pl.when(slab > 0)
            def _():
                sweep_copy(k, b).wait_recv()

            scale = cpl[pl.ds(b * B, B), :]
            field = jnp.concatenate(
                [right[p] - scale * Z[k, b, p].astype(F32) for p in range(2)], axis=0
            )
            high = field.astype(BF)
            low = (field - high.astype(F32)).astype(BF)
            state = dot(AH[b], low) + dot(AL[b], high) + dot(AH[b], high)
            for p in range(2):
                piece = state[p * B:(p + 1) * B]
                G[k, p, 0, b, 0] = piece.astype(BF)
                Y[k, p, pl.ds(b * B, B), :] = piece

            @pl.when(slab < slabs - 1)
            def _():
                sweep_copy(k, b).start()

            for p in range(2):
                for m in ((0, 4), (3, 1))[b]:
                    ag_copy(k, p, 0, m).start()
        root_back(k).start()

    def ag_forward(k, phase):
        for m in (0, 3):
            for p in range(2):
                ag_copy(k, p, phase, m).wait_recv()
                ag_copy(k, p, phase, m + 2).start()

    def ag_turn(k):
        for p in range(2):
            for m in (1, 4, 2, 5):
                ag_copy(k, p, 0, m).wait_recv()
        for m in (0, 3, 1, 4):
            for p in range(2):
                ag_copy(k, p, 1, m).start()

    def pick(k):
        for p in range(2):
            for m in (1, 4, 2, 5):
                ag_copy(k, p, 1, m).wait_recv()
        part_copy(k).wait_send()

        def slot(q, carry):
            rx, ry = q // RING, q % RING
            v = jnp.concatenate(
                [
                    jnp.concatenate([G[k, 0, rx, 0, ry], G[k, 1, ry, 0, rx]], axis=1),
                    jnp.concatenate([G[k, 0, rx, 1, ry], G[k, 1, ry, 1, rx]], axis=1),
                ],
                axis=0,
            )
            e = dot(TT[q], v).astype(BF)
            STAGE[q, 0] = e[:B, :C]
            STAGE[q, 1] = e[:B, C:]
            SND[k, q, 0] = e[B:, :C]
            SND[k, q, 1] = e[B:, C:]
            return carry

        lax.fori_loop(0, SLOTS, slot, 0, unroll=2)
        pick_copy(k).start()

    def back(k):
        pick_copy(k).wait_recv()

        def put(q, carry):
            STAGE[SLOTS + q] = RCB[k, q]
            return carry

        lax.fori_loop(0, SLOTS, put, 0, unroll=2)

        def leaf(l, carry):
            s = leaf_slot[l]
            v = jnp.concatenate([STAGE[s, 0], STAGE[s, 1]], axis=0)
            w = dot(OFFT[l], v).astype(BF)
            u = dot(widened(inv[0, l, 0], inv[0, l, 1]), w)
            X[k, 0, l] = (X[k, 0, l].astype(F32) - u[:B]).astype(BF)
            X[k, 1, l] = (X[k, 1, l].astype(F32) - u[B:]).astype(BF)
            return carry

        lax.fori_loop(0, LEAF, leaf, 0, unroll=2)
        sol_back(k).start()

    lag = slab * LAG_NUM // LAG_DEN

    def step(j, carry):
        def run(op, shift, *rest):
            k = j - shift

            @pl.when((k >= 0) & (k < chunks))
            def _():
                op(k, *rest)

        run(fwd, 0)

        @pl.when(j == 1)
        def _():
            setup_tables()

        run(expand, 1)
        run(rs_relay_first, 2)

        @pl.when(j == 4)
        def _():
            setup_transposed()

        run(rs_turn, 3)
        run(rs_relay_second, 4)
        run(sweep, 5 + lag)
        run(ag_forward, 6 + lag, 0)
        run(ag_turn, 7 + lag)
        run(ag_forward, 8 + lag, 1)
        run(back, 10 + lag)
        run(pick, 9 + lag)
        return carry

    lax.fori_loop(0, chunks + STEPS_AFTER + (slabs - 1) * LAG_NUM // LAG_DEN, step, 0)

    ids_copy().wait_send()

    def drain(k, carry):
        sol_back(k).wait()
        root_back(k).wait()
        for phase in range(2):
            for p in range(2):
                for m in range(6):
                    rs_copy(k, p, phase, m).wait_send()
                    ag_copy(k, p, phase, m).wait_send()
        for b in range(2):
            @pl.when(slab < slabs - 1)
            def _():
                sweep_copy(k, b).wait_send()
        pick_copy(k).wait_send()
        return carry

    lax.fori_loop(0, chunks, drain, 0)


def body(leaf_rhs, leaf_inv, leaf_off, parent, ancestors, root_rhs, root_inv, coupling):
    owners = parent[0, :, 0]
    anc = ancestors[0]
    width = leaf_rhs.shape[-1]
    chunks = width // C
    front = lax.axis_index("front")
    core, chip = front % 2, front // 2
    cx, cy = chip % RING, chip // RING
    n = jnp.arange(2 * SLOTS, dtype=jnp.int32)
    cls, q = n // SLOTS, n % SLOTS
    dest_x = (cx + q // RING) % RING
    dest_y = (cy + q % RING) % RING
    dest = (dest_y * RING + dest_x) * 2 + (core + cls) % 2
    match = (owners[None, :] == dest[:, None]).astype(jnp.int32)
    slot_leaf = jnp.sum(match * jnp.arange(LEAF, dtype=jnp.int32)[None, :], axis=1)
    leaf_slot = jnp.sum(match * n[:, None], axis=0)
    ids = jnp.sum(match[:, :, None] * (anc[None] + 1), axis=1) - 1
    ids = ids.reshape(2, SLOTS, B)
    cpl = jnp.broadcast_to(coupling[0][:, None], (2 * B, C))
    vmem = pl.BlockSpec(memory_space=pltpu.VMEM)
    smem = pl.BlockSpec(memory_space=pltpu.SMEM)
    hbm = pl.BlockSpec(memory_space=pl.ANY)
    scratch = [
        pltpu.VMEM((chunks, 2, LEAF, B, C), BF),
        pltpu.VMEM((2, LEAF, 2, B, C), BF),
        pltpu.VMEM((chunks, SLOTS, 2, B, C), BF),
        pltpu.VMEM((chunks, SLOTS, 2, B, C), BF),
        pltpu.VMEM((SLOTS, B), jnp.int32),
        pltpu.VMEM((SLOTS, 2 * B, 2 * B), BF),
        pltpu.VMEM((SLOTS, 2 * B, 2 * B), BF),
        pltpu.VMEM((LEAF, 2 * B, 2 * B), BF),
        pltpu.VMEM((chunks, 2, RING, 2, RING, B, C), BF),
        pltpu.VMEM((chunks, 2, 2, RING, B, C), BF),
        pltpu.VMEM((chunks, 2, 2, 2, RING, B, C), BF),
        pltpu.VMEM((chunks, 2, RING, 2, B, C), BF),
        pltpu.VMEM((chunks, 2, 2, B, C), BF),
        pltpu.VMEM((chunks, 2, 2, 2, B, C), BF),
        pltpu.VMEM((chunks, 2, 2 * B, C), BF),
        pltpu.VMEM((2, 2 * B, 2 * B), BF),
        pltpu.VMEM((2, 2 * B, 2 * B), BF),
        pltpu.VMEM((chunks, 2, 2, B, C), BF),
        pltpu.VMEM((chunks, 2, 2 * B, C), F32),
        pltpu.VMEM((chunks, 2, RING, 2, RING, B, C), BF),
        pltpu.VMEM((chunks, SLOTS, 2, B, C), BF),
        pltpu.VMEM((2 * SLOTS, 2, B, C), BF),
        pltpu.SemaphoreType.DMA((chunks, MESSAGES)),
        pltpu.SemaphoreType.DMA((chunks, MESSAGES)),
        pltpu.SemaphoreType.DMA((2,)),
        pltpu.SemaphoreType.DMA((chunks,)),
        pltpu.SemaphoreType.DMA((chunks,)),
        pltpu.SemaphoreType.DMA((chunks,)),
        pltpu.SemaphoreType.DMA((chunks,)),
    ]
    return pl.pallas_call(
        kernel,
        out_shape=(
            jax.ShapeDtypeStruct(leaf_rhs.shape, BF),
            jax.ShapeDtypeStruct(root_rhs.shape, F32),
        ),
        in_specs=[smem, smem, hbm, vmem, vmem, vmem, hbm, vmem, vmem],
        out_specs=(hbm, hbm),
        scratch_shapes=scratch,
        compiler_params=pltpu.CompilerParams(
            collective_id=0, has_side_effects=True, vmem_limit_bytes=67043328
        ),
        name="sweep_all",
    )(slot_leaf, leaf_slot, leaf_rhs, leaf_inv, leaf_off, ids, root_rhs, root_inv, cpl)


def solution(mesh):
    in_specs = (
        P("slab", None, "front", None, None),
        P("slab", "front", None, None, None),
        P("slab", "front", None, None, None),
        P("slab", "front", None),
        P("slab", "front", None),
        P("slab", None, "front", None),
        P("slab", "front", None, None, None),
        P("slab", "front"),
    )
    out_specs = (P("slab", None, "front", None, None), P("slab", None, "front", None))
    return jax.shard_map(body, mesh=mesh, in_specs=in_specs, out_specs=out_specs, check_vma=False)
```

time: 573 us -> 161 us (0.28)
  the two profiles are of different devices: /device:TPU:129 before, /device:TPU:225 now
where the time goes in v1:
time: 161 us; the launch traced here: 160 us
  Pallas kernels  149 us (93%)
  local copies, waits for them, and re-layouts  7.21 us (4%)
  other arithmetic  3.63 us (2%)
    pallas_call x1, Pallas kernels, body(): pl.pallas_call(kernel, out_shape=(jax.ShapeDtypeStruct(leaf_rhs.shape, BF...  149 us
    unnamed x4, local copies, waits for them, and re-layouts  5.7 us

profile of v1, /device:TPU:225, one launch (start us, length us, event | category | flops | bytes accessed | tf_op | source)
XLA Modules:
  0.0 160.4 jit_solution(2441919122347466023)
XLA Ops:
  0.7 1.4 fusion.1
  2.1 0.7 compare_convert_fusion
  2.9 0.1 copy.10
  2.9 0.7 add_bitcast_fusion
  3.6 0.1 multiply_reduce_fusion
  3.8 0.6 broadcast_add_fusion
  4.4 1.4 broadcast_in_dim.5.cpl
  5.8 148.9 %sweep_all.1 = (bf16[1,2,16,128,512]{4,3,2,1,0:T(8,128)(2,1)}, f32[1,2,256,512]{3,2,1,0:T(8,128)}) custom-call(s32[32]{0:T(128)} %get-tuple-element.3.slot_leaf, s32[16]{0:T(128)} %get-tuple-element.2.leaf_slot, bf16[1,2,16,128,512]{4,3,2,1,0:T(8,128)(2,1)} %rhs.1, bf16[1,16,2,128,128]{4,3,2,1,0:T(8,128)(2,1)} %inv.1, bf16[1,16,2,128,128]{4,3,2,1,0:T(8,128)(2,1)} %off.1, ...), custom_call_target="tpu_custom_call" | custom-call | tf_op jit(solution)/shard_map/sweep_all/pallas_call | solution.py:457
  154.7 0.0 copy-start
  154.7 4.7 %copy.13 = bf16[1,2,16,128,512]{4,3,2,1,0:T(8,128)(2,1)} copy(bf16[1,2,16,128,512]{4,3,2,1,0:T(8,128)(2,1)} %get-tuple-element.6) | data formatting | bytes 8388608
  159.5 0.0 copy-done
  159.5 1.0 copy.14
  (1 shorter events, 0.0 us)
Async XLA Ops:
  154.7 4.7 %copy-start = (f32[1,2,256,512]{3,2,1,0:T(8,128)S(1)}, f32[1,2,256,512]{3,2,1,0:T(8,128)}, u32[]{:S(2)}) copy-start(f32[1,2,256,512]{3,2,1,0:T(8,128)} %get-tuple-element.7) | copy-start | bytes 3145732

commit v2 on v1

--- a/solution.py
+++ b/solution.py
@@ -13,8 +13,9 @@
 RING = 4
 SLOTS = RING * RING
 MESSAGES = 52
-LAG_NUM, LAG_DEN = 3, 8
-STEPS_AFTER = 10
+LAG_NUM, LAG_ADD, LAG_DEN = 2, 5, 7
+GATHER = (6, 7, 8)
+WIDE = 8
 
 
 def dot(a, b):
@@ -28,10 +29,11 @@
 
 
 def kernel(
-    slot_leaf, leaf_slot, rhs, inv, off, ids, root_rhs, root_inv, cpl,
+    owners, rhs, inv_in, off_in, anc, root_rhs, root_inv, coupling,
     sol_out, root_out,
+    slot_leaf, leaf_slot, ids, inv, off, cpl,
     X, PART, SND, RCV, IDR, T, TT, OFFT, E, A1, F1, R1, A2, F2, RR, AH, AL, Z, Y, G, RCB, STAGE,
-    ssem, rsem, idsem, insem, rrsem, outsem, rootsem,
+    ssem, rsem, idsem, insem, rrsem, outsem, rootsem, matsem,
 ):
     slabs = lax.axis_size("slab")
     chunks = X.shape[0]
@@ -73,9 +75,44 @@
     def root_back(k):
         return pltpu.make_async_copy(Y.at[k], root_out.at[0, :, :, cols(k)], rootsem.at[k])
 
+    def matrices_in():
+        return (
+            pltpu.make_async_copy(inv_in, inv, matsem.at[0]),
+            pltpu.make_async_copy(off_in, off, matsem.at[1]),
+        )
+
     for k in range(chunks):
         rhs_in(k).start()
+        if k == 0:
+            for copy in matrices_in():
+                copy.start()
+    for k in range(chunks):
         root_rhs_in(k).start()
+
+    def find(l, carry):
+        f = owners[l]
+        rx = (((f >> 1) & 3) - cx) & 3
+        ry = ((f >> 3) - cy) & 3
+        leaf_slot[l] = (((f & 1) + core) & 1) * SLOTS + rx * RING + ry
+        return carry
+
+    lax.fori_loop(0, LEAF, find, 0)
+
+    def invert(q, carry):
+        for cls in range(2):
+            found = jnp.int32(0)
+            for l in range(LEAF):
+                found = jnp.where(leaf_slot[l] == cls * SLOTS + q, l + 1, found)
+            present = jnp.minimum(found, 1)
+            leaf = jnp.maximum(found - 1, 0)
+            slot_leaf[cls * SLOTS + q] = leaf
+            ids[cls, pl.ds(q, 1), :] = anc[0, pl.ds(leaf, 1), :] * present + (present - 1)
+        return carry
+
+    lax.fori_loop(0, SLOTS, invert, 0)
+    for b in range(2):
+        row = jnp.broadcast_to(coupling[:, b * B:(b + 1) * B], (B, B))
+        cpl[pl.ds(b * B, B), :] = row.T
 
     def send(src, dst, k, m, device):
         return pltpu.make_async_remote_copy(
@@ -146,20 +183,27 @@
         AL[b] = (full - high.astype(F32)).astype(BF)
 
     def fwd(k):
+        @pl.when(k == 0)
+        def _():
+            for copy in matrices_in():
+                copy.wait()
+
         rhs_in(k).wait()
         par = k % 2
 
-        def leaf(l, carry):
-            v = jnp.concatenate([X[k, 0, l], X[k, 1, l]], axis=0)
-            f = dot(widened(inv[0, l, 0], inv[0, l, 1]), v).astype(BF)
-            X[k, 0, l] = f[:B]
-            X[k, 1, l] = f[B:]
-            w = dot(widened(off[0, l, 0], off[0, l, 1]), f).astype(BF)
-            PART[par, l, 0] = w[:B]
-            PART[par, l, 1] = w[B:]
-            return carry
-
-        lax.fori_loop(0, LEAF, leaf, 0, unroll=2)
+        def leaves(g, carry):
+            ls = [g * WIDE + i for i in range(WIDE)]
+            v = [jnp.concatenate([X[k, 0, l], X[k, 1, l]], axis=0) for l in ls]
+            f = [dot(widened(inv[0, l, 0], inv[0, l, 1]), a).astype(BF) for l, a in zip(ls, v)]
+            w = [dot(widened(off[0, l, 0], off[0, l, 1]), a).astype(BF) for l, a in zip(ls, f)]
+            for l, a, b in zip(ls, f, w):
+                X[k, 0, l] = a[:B]
+                X[k, 1, l] = a[B:]
+                PART[par, l, 0] = b[:B]
+                PART[par, l, 1] = b[B:]
+            return carry
+
+        lax.fori_loop(0, LEAF // WIDE, leaves, 0)
 
         def put(q, carry):
             SND[k, q] = PART[par, slot_leaf[SLOTS + q]]
@@ -191,24 +235,23 @@
         part_copy(k).wait_recv()
         par = k % 2
 
-        def slot(q, carry):
-            rx, ry = q // RING, q % RING
-            leaf = slot_leaf[q]
-            v = jnp.concatenate(
-                [
-                    jnp.concatenate([PART[par, leaf, 0], PART[par, leaf, 1]], axis=1),
-                    jnp.concatenate([RCV[k, q, 0], RCV[k, q, 1]], axis=1),
-                ],
-                axis=0,
-            )
-            e = dot(T[q], v).astype(BF)
-            E[k, 0, rx, 0, ry] = e[:B, :C]
-            E[k, 0, rx, 1, ry] = e[B:, :C]
-            E[k, 1, ry, 0, rx] = e[:B, C:]
-            E[k, 1, ry, 1, rx] = e[B:, C:]
-            return carry
-
-        lax.fori_loop(0, SLOTS, slot, 0, unroll=2)
+        def slots(rx, carry):
+            v = []
+            for ry in range(RING):
+                q = rx * RING + ry
+                leaf = slot_leaf[q]
+                mine = jnp.concatenate([PART[par, leaf, 0], PART[par, leaf, 1]], axis=1)
+                other = jnp.concatenate([RCV[k, q, 0], RCV[k, q, 1]], axis=1)
+                v.append(jnp.concatenate([mine, other], axis=0))
+            e = [dot(T[rx * RING + ry], a).astype(BF) for ry, a in enumerate(v)]
+            for ry, a in enumerate(e):
+                E[k, 0, rx, 0, ry] = a[:B, :C]
+                E[k, 0, rx, 1, ry] = a[B:, :C]
+                E[k, 1, ry, 0, rx] = a[:B, C:]
+                E[k, 1, ry, 1, rx] = a[B:, C:]
+            return carry
+
+        lax.fori_loop(0, RING, slots, 0)
         for m in (0, 3, 1, 4):
             for p in range(2):
                 rs_copy(k, p, 0, m).start()
@@ -281,10 +324,12 @@
             def _():
                 sweep_copy(k, b).start()
 
-            for p in range(2):
-                for m in ((0, 4), (3, 1))[b]:
-                    ag_copy(k, p, 0, m).start()
         root_back(k).start()
+
+    def ag_send(k):
+        for m in (0, 3, 1, 4):
+            for p in range(2):
+                ag_copy(k, p, 0, m).start()
 
     def ag_forward(k, phase):
         for m in (0, 3):
@@ -306,47 +351,55 @@
                 ag_copy(k, p, 1, m).wait_recv()
         part_copy(k).wait_send()
 
-        def slot(q, carry):
-            rx, ry = q // RING, q % RING
-            v = jnp.concatenate(
-                [
-                    jnp.concatenate([G[k, 0, rx, 0, ry], G[k, 1, ry, 0, rx]], axis=1),
-                    jnp.concatenate([G[k, 0, rx, 1, ry], G[k, 1, ry, 1, rx]], axis=1),
-                ],
-                axis=0,
-            )
-            e = dot(TT[q], v).astype(BF)
-            STAGE[q, 0] = e[:B, :C]
-            STAGE[q, 1] = e[:B, C:]
-            SND[k, q, 0] = e[B:, :C]
-            SND[k, q, 1] = e[B:, C:]
-            return carry
-
-        lax.fori_loop(0, SLOTS, slot, 0, unroll=2)
+        def slots(rx, carry):
+            v = []
+            for ry in range(RING):
+                top = jnp.concatenate([G[k, 0, rx, 0, ry], G[k, 1, ry, 0, rx]], axis=1)
+                low = jnp.concatenate([G[k, 0, rx, 1, ry], G[k, 1, ry, 1, rx]], axis=1)
+                v.append(jnp.concatenate([top, low], axis=0))
+            e = [dot(TT[rx * RING + ry], a).astype(BF) for ry, a in enumerate(v)]
+            for ry, a in enumerate(e):
+                q = rx * RING + ry
+                STAGE[k % 2, q, 0] = a[:B, :C]
+                STAGE[k % 2, q, 1] = a[:B, C:]
+                SND[k, q, 0] = a[B:, :C]
+                SND[k, q, 1] = a[B:, C:]
+            return carry
+
+        lax.fori_loop(0, RING, slots, 0)
         pick_copy(k).start()
 
     def back(k):
         pick_copy(k).wait_recv()
 
         def put(q, carry):
-            STAGE[SLOTS + q] = RCB[k, q]
+            STAGE[k % 2, SLOTS + q] = RCB[k, q]
             return carry
 
         lax.fori_loop(0, SLOTS, put, 0, unroll=2)
 
-        def leaf(l, carry):
-            s = leaf_slot[l]
-            v = jnp.concatenate([STAGE[s, 0], STAGE[s, 1]], axis=0)
-            w = dot(OFFT[l], v).astype(BF)
-            u = dot(widened(inv[0, l, 0], inv[0, l, 1]), w)
-            X[k, 0, l] = (X[k, 0, l].astype(F32) - u[:B]).astype(BF)
-            X[k, 1, l] = (X[k, 1, l].astype(F32) - u[B:]).astype(BF)
-            return carry
-
-        lax.fori_loop(0, LEAF, leaf, 0, unroll=2)
+        def leaves(g, carry):
+            ls = [g * WIDE + i for i in range(WIDE)]
+            ss = [leaf_slot[l] for l in ls]
+            v = [jnp.concatenate([STAGE[k % 2, n, 0], STAGE[k % 2, n, 1]], axis=0) for n in ss]
+            f = [jnp.concatenate([X[k, 0, l], X[k, 1, l]], axis=0).astype(F32) for l in ls]
+            w = [dot(OFFT[l], a).astype(BF) for l, a in zip(ls, v)]
+            u = [dot(widened(inv[0, l, 0], inv[0, l, 1]), a) for l, a in zip(ls, w)]
+            for l, a, b in zip(ls, f, u):
+                r = (a - b).astype(BF)
+                X[k, 0, l] = r[:B]
+                X[k, 1, l] = r[B:]
+            return carry
+
+        lax.fori_loop(0, LEAF // WIDE, leaves, 0)
         sol_back(k).start()
 
-    lag = slab * LAG_NUM // LAG_DEN
+    lag = (slab * LAG_NUM + LAG_ADD) // LAG_DEN
+    sw = 5 + lag
+    g1 = jnp.maximum(GATHER[0], sw)
+    g2 = jnp.maximum(GATHER[1], sw)
+    g3 = jnp.maximum(GATHER[2], sw + 1)
+    last = max(GATHER[2], 6 + ((slabs - 1) * LAG_NUM + LAG_ADD) // LAG_DEN)
 
     def step(j, carry):
         def run(op, shift, *rest):
@@ -371,15 +424,16 @@
 
         run(rs_turn, 3)
         run(rs_relay_second, 4)
-        run(sweep, 5 + lag)
-        run(ag_forward, 6 + lag, 0)
-        run(ag_turn, 7 + lag)
-        run(ag_forward, 8 + lag, 1)
-        run(back, 10 + lag)
-        run(pick, 9 + lag)
+        run(sweep, sw)
+        run(ag_send, g1)
+        run(ag_turn, g3)
+        run(ag_forward, g2, 0)
+        run(ag_forward, g3, 1)
+        run(pick, g3 + 1)
+        run(back, g3 + 2)
         return carry
 
-    lax.fori_loop(0, chunks + STEPS_AFTER + (slabs - 1) * LAG_NUM // LAG_DEN, step, 0)
+    lax.fori_loop(0, chunks + last + 2, step, 0)
 
     ids_copy().wait_send()
 
@@ -402,28 +456,19 @@
 
 
 def body(leaf_rhs, leaf_inv, leaf_off, parent, ancestors, root_rhs, root_inv, coupling):
-    owners = parent[0, :, 0]
-    anc = ancestors[0]
+    owners = parent.reshape(LEAF)
     width = leaf_rhs.shape[-1]
     chunks = width // C
-    front = lax.axis_index("front")
-    core, chip = front % 2, front // 2
-    cx, cy = chip % RING, chip // RING
-    n = jnp.arange(2 * SLOTS, dtype=jnp.int32)
-    cls, q = n // SLOTS, n % SLOTS
-    dest_x = (cx + q // RING) % RING
-    dest_y = (cy + q % RING) % RING
-    dest = (dest_y * RING + dest_x) * 2 + (core + cls) % 2
-    match = (owners[None, :] == dest[:, None]).astype(jnp.int32)
-    slot_leaf = jnp.sum(match * jnp.arange(LEAF, dtype=jnp.int32)[None, :], axis=1)
-    leaf_slot = jnp.sum(match * n[:, None], axis=0)
-    ids = jnp.sum(match[:, :, None] * (anc[None] + 1), axis=1) - 1
-    ids = ids.reshape(2, SLOTS, B)
-    cpl = jnp.broadcast_to(coupling[0][:, None], (2 * B, C))
     vmem = pl.BlockSpec(memory_space=pltpu.VMEM)
     smem = pl.BlockSpec(memory_space=pltpu.SMEM)
     hbm = pl.BlockSpec(memory_space=pl.ANY)
     scratch = [
+        pltpu.SMEM((2 * SLOTS,), jnp.int32),
+        pltpu.SMEM((LEAF,), jnp.int32),
+        pltpu.VMEM((2, SLOTS, B), jnp.int32),
+        pltpu.VMEM((1, LEAF, 2, B, B), BF),
+        pltpu.VMEM((1, LEAF, 2, B, B), BF),
+        pltpu.VMEM((2 * B, C), F32),
         pltpu.VMEM((chunks, 2, LEAF, B, C), BF),
         pltpu.VMEM((2, LEAF, 2, B, C), BF),
         pltpu.VMEM((chunks, SLOTS, 2, B, C), BF),
@@ -445,7 +490,7 @@
         pltpu.VMEM((chunks, 2, 2 * B, C), F32),
         pltpu.VMEM((chunks, 2, RING, 2, RING, B, C), BF),
         pltpu.VMEM((chunks, SLOTS, 2, B, C), BF),
-        pltpu.VMEM((2 * SLOTS, 2, B, C), BF),
+        pltpu.VMEM((2, 2 * SLOTS, 2, B, C), BF),
         pltpu.SemaphoreType.DMA((chunks, MESSAGES)),
         pltpu.SemaphoreType.DMA((chunks, MESSAGES)),
         pltpu.SemaphoreType.DMA((2,)),
@@ -453,6 +498,7 @@
         pltpu.SemaphoreType.DMA((chunks,)),
         pltpu.SemaphoreType.DMA((chunks,)),
         pltpu.SemaphoreType.DMA((chunks,)),
+        pltpu.SemaphoreType.DMA((2,)),
     ]
     return pl.pallas_call(
         kernel,
@@ -460,14 +506,14 @@
             jax.ShapeDtypeStruct(leaf_rhs.shape, BF),
             jax.ShapeDtypeStruct(root_rhs.shape, F32),
         ),
-        in_specs=[smem, smem, hbm, vmem, vmem, vmem, hbm, vmem, vmem],
+        in_specs=[smem, hbm, hbm, hbm, vmem, hbm, vmem, vmem],
         out_specs=(hbm, hbm),
         scratch_shapes=scratch,
         compiler_params=pltpu.CompilerParams(
             collective_id=0, has_side_effects=True, vmem_limit_bytes=67043328
         ),
         name="sweep_all",
-    )(slot_leaf, leaf_slot, leaf_rhs, leaf_inv, leaf_off, ids, root_rhs, root_inv, cpl)
+    )(owners, leaf_rhs, leaf_inv, leaf_off, ancestors, root_rhs, root_inv, coupling)
 
 
 def solution(mesh):

time: 161 us -> 139 us (0.86)
  Pallas kernels: 149 us -> 132 us
  other arithmetic: 3.63 us -> 0 us
    pallas_call x1, Pallas kernels: 149 us -> 132 us  [body(): pl.pallas_call(kernel, out_shape=(jax.ShapeDtypeStruct(leaf_rhs.shape, BF...]
where the time goes in v2:
time: 139 us; the launch traced here: 138 us
  Pallas kernels  132 us (95%)
  local copies, waits for them, and re-layouts  5.7 us (4%)
    pallas_call x1, Pallas kernels, body(): pl.pallas_call(kernel, out_shape=(jax.ShapeDtypeStruct(leaf_rhs.shape, BF...  132 us
    unnamed x4, local copies, waits for them, and re-layouts  5.7 us

profile of v2, /device:TPU:225, one launch (start us, length us, event | category | flops | bytes accessed | tf_op | source)
XLA Modules:
  0.0 138.5 jit_solution(11016927670572372732)
XLA Ops:
  0.6 132.1 %sweep_all.1 = (bf16[1,2,16,128,512]{4,3,2,1,0:T(8,128)(2,1)}, f32[1,2,256,512]{3,2,1,0:T(8,128)}) custom-call(s32[16]{0:T(128)} %bitcast.1, bf16[1,2,16,128,512]{4,3,2,1,0:T(8,128)(2,1)} %rhs.1, bf16[1,16,2,128,128]{4,3,2,1,0:T(8,128)(2,1)} %inv_in.1, bf16[1,16,2,128,128]{4,3,2,1,0:T(8,128)(2,1)} %off_in.1, s32[1,16,128]{2,1,0:T(8,128)} %anc.1, ...), custom_call_target="tpu_custom_call" | custom-call | tf_op jit(solution)/shard_map/sweep_all/pallas_call | solution.py:503
  132.7 0.0 copy-start
  132.8 4.7 %copy.12 = bf16[1,2,16,128,512]{4,3,2,1,0:T(8,128)(2,1)} copy(bf16[1,2,16,128,512]{4,3,2,1,0:T(8,128)(2,1)} %get-tuple-element.4) | data formatting | bytes 8388608
  137.5 0.0 copy-done
  137.5 1.0 copy.13
Async XLA Ops:
  132.7 4.7 %copy-start = (f32[1,2,256,512]{3,2,1,0:T(8,128)S(1)}, f32[1,2,256,512]{3,2,1,0:T(8,128)}, u32[]{:S(2)}) copy-start(f32[1,2,256,512]{3,2,1,0:T(8,128)} %get-tuple-element.5) | copy-start | bytes 3145732

commit v3 on v2

--- a/solution.py
+++ b/solution.py
@@ -12,9 +12,10 @@
 LEAF = 16
 RING = 4
 SLOTS = RING * RING
-MESSAGES = 52
+MESSAGES = 54
+HALF = SLOTS // 2
 LAG_NUM, LAG_ADD, LAG_DEN = 2, 5, 7
-GATHER = (6, 7, 8)
+GATHER = (5, 6, 8)
 WIDE = 8
 
 
@@ -126,8 +127,9 @@
             device_id=partner, device_id_type=pl.DeviceIdType.MESH,
         )
 
-    def part_copy(k):
-        return send(SND.at[k], RCV.at[k], k, 0, partner)
+    def part_copy(k, h):
+        some = pl.ds(h * HALF, HALF)
+        return send(SND.at[k, some], RCV.at[k, some], k, (0, 52)[h], partner)
 
     def rs_copy(k, p, phase, m):
         nxt, prv = ways[p if phase == 0 else 1 - p]
@@ -166,8 +168,9 @@
         )[m]
         return send(s, d, k, 27 + phase * 12 + p * 6 + m, device)
 
-    def pick_copy(k):
-        return send(SND.at[k], RCB.at[k], k, 51, partner)
+    def pick_copy(k, h):
+        some = pl.ds(h * HALF, HALF)
+        return send(SND.at[k, some], RCB.at[k, some], k, (51, 53)[h], partner)
 
     @pl.when(slab == 0)
     def _():
@@ -209,8 +212,9 @@
             SND[k, q] = PART[par, slot_leaf[SLOTS + q]]
             return carry
 
-        lax.fori_loop(0, SLOTS, put, 0, unroll=2)
-        part_copy(k).start()
+        for h in range(2):
+            lax.fori_loop(h * HALF, (h + 1) * HALF, put, 0, unroll=2)
+            part_copy(k, h).start()
 
     def setup_tables():
         ids_copy().wait_recv()
@@ -232,7 +236,6 @@
         lax.fori_loop(0, SLOTS, table, 0)
 
     def expand(k):
-        part_copy(k).wait_recv()
         par = k % 2
 
         def slots(rx, carry):
@@ -251,7 +254,9 @@
                 E[k, 1, ry, 1, rx] = a[B:, C:]
             return carry
 
-        lax.fori_loop(0, RING, slots, 0)
+        for h in range(2):
+            part_copy(k, h).wait_recv()
+            lax.fori_loop(h * 2, h * 2 + 2, slots, 0)
         for m in (0, 3, 1, 4):
             for p in range(2):
                 rs_copy(k, p, 0, m).start()
@@ -294,36 +299,41 @@
         for p in range(2):
             for m in (1, 4, 2, 5):
                 rs_copy(k, p, 1, m).wait_recv()
+        right = [
+            RR[k, p, pl.ds(b * B, B), :].astype(F32)
+            - (
+                R1[k, p, 0, b].astype(F32)
+                + F2[k, p, 0, b].astype(F32)
+                + F2[k, p, 1, b].astype(F32)
+            )
+            for b in range(2)
+            for p in range(2)
+        ]
+        states = []
         for b in range(2):
-            right = []
-            for p in range(2):
-                total = (
-                    R1[k, p, 0, b].astype(F32)
-                    + F2[k, p, 0, b].astype(F32)
-                    + F2[k, p, 1, b].astype(F32)
-                )
-                right.append(RR[k, p, pl.ds(b * B, B), :].astype(F32) - total)
+            scale = cpl[pl.ds(b * B, B), :]
 
             @pl.when(slab > 0)
             def _():
                 sweep_copy(k, b).wait_recv()
 
-            scale = cpl[pl.ds(b * B, B), :]
             field = jnp.concatenate(
-                [right[p] - scale * Z[k, b, p].astype(F32) for p in range(2)], axis=0
+                [right[2 * b + p] - scale * Z[k, b, p].astype(F32) for p in range(2)], axis=0
             )
             high = field.astype(BF)
             low = (field - high.astype(F32)).astype(BF)
             state = dot(AH[b], low) + dot(AL[b], high) + dot(AH[b], high)
-            for p in range(2):
-                piece = state[p * B:(p + 1) * B]
-                G[k, p, 0, b, 0] = piece.astype(BF)
-                Y[k, p, pl.ds(b * B, B), :] = piece
+            states.append(state)
+            for p in range(2):
+                G[k, p, 0, b, 0] = state[p * B:(p + 1) * B].astype(BF)
 
             @pl.when(slab < slabs - 1)
             def _():
                 sweep_copy(k, b).start()
 
+        for b in range(2):
+            for p in range(2):
+                Y[k, p, pl.ds(b * B, B), :] = states[b][p * B:(p + 1) * B]
         root_back(k).start()
 
     def ag_send(k):
@@ -349,7 +359,8 @@
         for p in range(2):
             for m in (1, 4, 2, 5):
                 ag_copy(k, p, 1, m).wait_recv()
-        part_copy(k).wait_send()
+        for h in range(2):
+            part_copy(k, h).wait_send()
 
         def slots(rx, carry):
             v = []
@@ -366,17 +377,18 @@
                 SND[k, q, 1] = a[B:, C:]
             return carry
 
-        lax.fori_loop(0, RING, slots, 0)
-        pick_copy(k).start()
+        for h in range(2):
+            lax.fori_loop(h * 2, h * 2 + 2, slots, 0)
+            pick_copy(k, h).start()
 
     def back(k):
-        pick_copy(k).wait_recv()
-
         def put(q, carry):
             STAGE[k % 2, SLOTS + q] = RCB[k, q]
             return carry
 
-        lax.fori_loop(0, SLOTS, put, 0, unroll=2)
+        for h in range(2):
+            pick_copy(k, h).wait_recv()
+            lax.fori_loop(h * HALF, (h + 1) * HALF, put, 0, unroll=2)
 
         def leaves(g, carry):
             ls = [g * WIDE + i for i in range(WIDE)]
@@ -449,7 +461,8 @@
             @pl.when(slab < slabs - 1)
             def _():
                 sweep_copy(k, b).wait_send()
-        pick_copy(k).wait_send()
+        for h in range(2):
+            pick_copy(k, h).wait_send()
         return carry
 
     lax.fori_loop(0, chunks, drain, 0)

time: 139 us -> 138 us (level)
  no operation moved by 1% of the time
where the time goes in v3:
time: 138 us
  Pallas kernels  132 us (96%)
  local copies, waits for them, and re-layouts  5.7 us (4%)
    pallas_call x1, Pallas kernels, body(): pl.pallas_call(kernel, out_shape=(jax.ShapeDtypeStruct(leaf_rhs.shape, BF...  132 us
    unnamed x4, local copies, waits for them, and re-layouts  5.7 us

profile of v3, /device:TPU:225, one launch (start us, length us, event | category | flops | bytes accessed | tf_op | source)
XLA Modules:
  0.0 138.3 jit_solution(14174955096643999776)
XLA Ops:
  0.6 132.0 %sweep_all.1 = (bf16[1,2,16,128,512]{4,3,2,1,0:T(8,128)(2,1)}, f32[1,2,256,512]{3,2,1,0:T(8,128)}) custom-call(s32[16]{0:T(128)} %bitcast.1, bf16[1,2,16,128,512]{4,3,2,1,0:T(8,128)(2,1)} %rhs.1, bf16[1,16,2,128,128]{4,3,2,1,0:T(8,128)(2,1)} %inv_in.1, bf16[1,16,2,128,128]{4,3,2,1,0:T(8,128)(2,1)} %off_in.1, s32[1,16,128]{2,1,0:T(8,128)} %anc.1, ...), custom_call_target="tpu_custom_call" | custom-call | tf_op jit(solution)/shard_map/sweep_all/pallas_call | solution.py:516
  132.6 0.0 copy-start
  132.6 4.7 %copy.12 = bf16[1,2,16,128,512]{4,3,2,1,0:T(8,128)(2,1)} copy(bf16[1,2,16,128,512]{4,3,2,1,0:T(8,128)(2,1)} %get-tuple-element.4) | data formatting | bytes 8388608
  137.3 0.0 copy-done
  137.3 1.0 copy.13
Async XLA Ops:
  132.6 4.7 %copy-start = (f32[1,2,256,512]{3,2,1,0:T(8,128)S(1)}, f32[1,2,256,512]{3,2,1,0:T(8,128)}, u32[]{:S(2)}) copy-start(f32[1,2,256,512]{3,2,1,0:T(8,128)} %get-tuple-element.5) | copy-start | bytes 3145732
